TPU v7x, 32 devices: a whole 2x2x4 slice. The times are simulated.
32 devices in a mesh: shape: 8 (over z, x), cls: 4 (over y, core).
Axes of the slice: x: 2, y: 2, z: 4, core: 2. Of those that a mesh axis runs over, the one named last changes fastest.
Arguments:
- shapes: bfloat16 [4096, 1280], P('shape', 'cls'), may hold values from -600 to 600
- classes: bfloat16 [20480, 1280], P('cls'), may hold values from -400 to 400
- counts: int32 [20480], P('cls'), may hold values from 0 to 2, as said below
Outputs:
- assignment: bfloat16 [4096, 20480], P('shape', 'cls')
Inputs may be any that keep to these rules, and one draw needn't show every extreme that they name: The counts sum to 4096; exactly 1024 classes have count 2.
All inputs are finite; a program needn't handle non-finite values.
Results may differ from a plain program's by a relative error of at most 0.001.
Values may be sent and summed in bfloat16 or wider, within the bound.
No kernel may reach another device: no remote copies, remote signals or barrier semaphores. Data moves between devices by JAX's collectives and lax.ppermute only.
A program may use at most 128 MiB of HBM per device.

v0:
```python
import jax
import jax.numpy as jnp
from jax import lax
from jax.sharding import PartitionSpec as P

ITERS = 3
logit_scale = 40.0
epsilon = 1e-06


def row_totals(partial_value):
    return lax.psum(partial_value, "cls")


def shards(shapes, classes, counts):
    class_f = classes.astype(jnp.float32)
    class_scale = lax.rsqrt(jnp.sum(class_f * class_f, axis=1) + epsilon)
    piece = lax.all_gather(shapes, "cls", axis=1, tiled=True)
    term = lax.dot_general(
        piece, classes, (((1,), (1,)), ((), ())), preferred_element_type=jnp.float32
    )
    piece_f = piece.astype(jnp.float32)
    squares = jnp.sum(piece_f * piece_f, axis=1)
    shape_scale = lax.rsqrt(squares + epsilon)
    kernel = jnp.exp(logit_scale * term * shape_scale[:, None] * class_scale[None, :])
    target = counts.astype(jnp.float32)
    row_inv = 1.0 / row_totals(jnp.sum(kernel, axis=1))
    col_scale = jnp.zeros((classes.shape[0],), jnp.float32)
    for step in range(ITERS):
        column_part = jnp.dot(row_inv, kernel, precision=lax.Precision.HIGHEST)
        col_scale = target / lax.psum(column_part, "shape")
        row_inv = 1.0 / row_totals(jnp.dot(kernel, col_scale, precision=lax.Precision.HIGHEST))
    result = row_inv[:, None] * kernel * col_scale[None, :]
    return result.astype(jnp.bfloat16)


def solution(mesh):
    placed = (P("shape", "cls"), P("cls", None), P("cls"))
    return jax.shard_map(
        shards, mesh=mesh, in_specs=placed, out_specs=P("shape", "cls"), check_vma=False
    )
```

profile of v0, /device:TPU:0, one launch (start us, length us, event | category | flops | bytes accessed | tf_op | source)
XLA Modules:
  0.0 246.2 jit_solution(15459654316340277970)
XLA Ops:
  6.5 0.0 all-gather.2.cloned.1.call-start
  6.5 0.7 all-gather.2.cloned.1.call-update
  7.3 7.3 %multiply_reduce_fusion = f32[5120]{0:T(1024)S(1)} fusion(bf16[5120,1280]{1,0:T(8,128)(2,1)} %param.4), kind=kLoop, calls=%fused_computation | loop fusion | flops 19655680 | bytes 13127680 | tf_op jit(solution)/shard_map/reduce_sum | solution.py:17
  14.6 15.2 %all-gather.2.cloned.1.call-done = bf16[512,1280]{0,1:T(8,128)(2,1)} async-done(((bf16[512,320]{0,1:T(8,128)(2,1)}), bf16[512,1280]{0,1:T(8,128)(2,1)}) %all-gather.2.cloned.1.call-update) | async-done | bytes 1310736 | tf_op jit(solution)/shard_map/all_gather | solution.py:18
  29.8 1.7 multiply_reduce_fusion.1
  31.5 16.2 %fusion = (f32[512]{0:T(512)S(1)}, f32[512,5120]{1,0:T(8,128)}) fusion(f32[5120]{0:T(1024)S(1)} %add_rsqrt_fusion, f32[512]{0:T(512)S(1)} %rsqrt_multiply_fusion, bf16[512,1280]{0,1:T(8,128)(2,1)} %all-gather.2.cloned.1.call-done, bf16[5120,1280]{1,0:T(8,128)(2,1)} %param.4), kind=kOutput, calls=%fused_computation.13 | convolution fusion | flops 6718750208 | bytes 24928256 | tf_op jit(solution)/shard_map/dot_general | solution.py:19
  47.7 0.0 copy-start
  47.7 5.9 %psum.49 = f32[512]{0:T(512)S(1)} all-reduce(f32[512]{0:T(512)S(1)} %get-tuple-element.5), channel_id=1, replica_groups=mesh['shape'=8,'cls'=4] {'cls'}, use_global_device_ids=true, to_apply=%region_3.0 | all-reduce | flops 512 | bytes 4096 | tf_op jit(solution)/shard_map/psum | solution.py:12
  53.5 7.6 %fusion.1 = f32[1,5120]{1,0:T(1,128)S(1)} fusion(f32[512,1]{0,1:T(1,128)S(1)} %bitcast.32, f32[512,5120]{1,0:T(8,128)} %get-tuple-element.6), kind=kOutput, calls=%fused_computation.14 | convolution fusion | flops 31457280 | bytes 10508288 | tf_op jit(solution)/shard_map/dot_general | solution.py:30
  61.2 37.2 %psum.50 = f32[5120]{0:T(1024)S(1)} all-reduce(f32[5120]{0:T(1024)S(1)} %bitcast.27), channel_id=1, replica_groups=mesh['shape'=8,'cls'=4] {'shape'}, use_global_device_ids=true, to_apply=%region_4.0 | all-reduce | flops 5120 | bytes 40960 | tf_op jit(solution)/shard_map/psum | solution.py:31
  98.4 0.0 copy-done
  98.4 11.5 %fusion.2 = f32[1,512]{1,0:T(1,128)S(1)} fusion(f32[512,5120]{1,0:T(8,128)} %get-tuple-element.6, f32[5120,1]{0,1:T(1,128)S(1)} %bitcast.30), kind=kOutput, calls=%fused_computation.15 | convolution fusion | flops 31457280 | bytes 10508288 | tf_op jit(solution)/shard_map/dot_general | solution.py:32
  109.9 5.7 %psum.51 = f32[512]{0:T(512)S(1)} all-reduce(f32[512]{0:T(512)S(1)} %bitcast.33), channel_id=1, replica_groups=mesh['shape'=8,'cls'=4] {'cls'}, use_global_device_ids=true, to_apply=%region_5.0 | all-reduce | flops 512 | bytes 4096 | tf_op jit(solution)/shard_map/psum | solution.py:12
  115.6 7.6 %fusion.3 = f32[1,5120]{1,0:T(1,128)S(1)} fusion(f32[512,1]{0,1:T(1,128)S(1)} %bitcast.34, f32[512,5120]{1,0:T(8,128)} %get-tuple-element.6), kind=kOutput, calls=%fused_computation.16 | convolution fusion | flops 31457280 | bytes 10508288 | tf_op jit(solution)/shard_map/dot_general | solution.py:30
  123.2 33.0 %psum.52 = f32[5120]{0:T(1024)S(1)} all-reduce(f32[5120]{0:T(1024)S(1)} %bitcast.28), channel_id=1, replica_groups=mesh['shape'=8,'cls'=4] {'shape'}, use_global_device_ids=true, to_apply=%region_6.0 | all-reduce | flops 5120 | bytes 40960 | tf_op jit(solution)/shard_map/psum | solution.py:31
  156.2 11.5 %fusion.4 = f32[1,512]{1,0:T(1,128)S(1)} fusion(f32[512,5120]{1,0:T(8,128)} %get-tuple-element.6, f32[5120,1]{0,1:T(1,128)S(1)} %bitcast.31), kind=kOutput, calls=%fused_computation.17 | convolution fusion | flops 31457280 | bytes 10508288 | tf_op jit(solution)/shard_map/dot_general | solution.py:32
  167.7 5.9 %psum.53 = f32[512]{0:T(512)S(1)} all-reduce(f32[512]{0:T(512)S(1)} %bitcast.35), channel_id=1, replica_groups=mesh['shape'=8,'cls'=4] {'cls'}, use_global_device_ids=true, to_apply=%region_7.0 | all-reduce | flops 512 | bytes 4096 | tf_op jit(solution)/shard_map/psum | solution.py:12
  173.6 7.6 %fusion.5 = f32[1,5120]{1,0:T(1,128)S(1)} fusion(f32[512,1]{0,1:T(1,128)S(1)} %bitcast.36, f32[512,5120]{1,0:T(8,128)} %get-tuple-element.6), kind=kOutput, calls=%fused_computation.18 | convolution fusion | flops 31457280 | bytes 10508288 | tf_op jit(solution)/shard_map/dot_general | solution.py:30
  181.2 33.0 %psum.54 = f32[5120]{0:T(1024)S(1)} all-reduce(f32[5120]{0:T(1024)S(1)} %bitcast.29), channel_id=1, replica_groups=mesh['shape'=8,'cls'=4] {'shape'}, use_global_device_ids=true, to_apply=%region_8.0 | all-reduce | flops 5120 | bytes 40960 | tf_op jit(solution)/shard_map/psum | solution.py:31
  214.2 11.5 %fusion.6 = f32[1,512]{1,0:T(1,128)S(1)} fusion(f32[512,5120]{1,0:T(8,128)} %get-tuple-element.6, f32[5120,1]{0,1:T(1,128)S(1)} %bitcast.26), kind=kOutput, calls=%fused_computation.19 | convolution fusion | flops 31457280 | bytes 10508288 | tf_op jit(solution)/shard_map/dot_general | solution.py:32
  225.7 5.7 %psum.55 = f32[512]{0:T(512)S(1)} all-reduce(f32[512]{0:T(512)S(1)} %bitcast.37), channel_id=1, replica_groups=mesh['shape'=8,'cls'=4] {'cls'}, use_global_device_ids=true, to_apply=%region_9.0 | all-reduce | flops 512 | bytes 4096 | tf_op jit(solution)/shard_map/psum | solution.py:12
  231.4 8.0 %multiply_convert_fusion = bf16[512,5120]{1,0:T(8,128)(2,1)} fusion(f32[512,5120]{1,0:T(8,128)} %get-tuple-element.6, f32[5120]{0:T(1024)S(1)} %convert_divide_fusion, f32[512]{0:T(512)S(1)} %broadcast_divide_fusion), kind=kLoop, calls=%fused_computation.1 | loop fusion | flops 7864320 | bytes 15751168 | tf_op jit(solution)/shard_map/convert_element_type | solution.py:34
  (9 shorter events, 0.1 us)
Async XLA Ops:
  6.5 23.3 %all-gather.2.cloned.1.call-start = ((), (), s32[]{:S(2)}) async-start(), calls=%async_computation | async-start | bytes 1638400 | tf_op jit(solution)/shard_map/all_gather | solution.py:18
  47.7 50.7 %copy-start = (s32[5120]{0:T(1024)S(1)}, s32[5120]{0:T(1024)}, u32[]{:S(2)}) copy-start(s32[5120]{0:T(1024)} %param.5) | copy-start | bytes 61444
Sparse Core Ops, SparseCore 0:
  8.9 20.8 all-gather.1
where the time goes:
time: 247 us; the launch traced here: 246 us
  blocking collectives  126 us (51%)
  matrix products  73.5 us (30%)
  other arithmetic  17.1 us (7%)
  waiting for transfers between devices  15.9 us (6%)
  between operations  13.4 us (5%)
    psum x3, blocking collectives, shards(): col_scale = target / lax.psum(column_part, 'shape')  103 us
    dot_general x3, matrix products, shards(): jnp.dot(kernel, col_scale, precision=lax.Precision.HIGHEST)  34.4 us
    psum x4, blocking collectives, row_totals(): return lax.psum(partial_value, 'cls')  23 us
    dot_general x3, matrix products, shards(): column_part = jnp.dot(row_inv, kernel, precision=lax.Precision.HIGHEST)  22.9 us
    dot_general x1, matrix products, shards(): lax.dot_general(piece, classes, (((1,), (1,)), ((), ())), preferred_eleme...  16.2 us
    all_gather x1, waiting for transfers between devices, shards(): piece = lax.all_gather(shapes, 'cls', axis=1, tiled=True)  15.2 us
    convert_element_type x1, other arithmetic, shards(): return result.astype(jnp.bfloat16)  8 us
    reduce_sum x1, other arithmetic, shards(): class_scale = lax.rsqrt(jnp.sum(class_f * class_f, axis=1) + epsilon)  7.35 us
  transfers between devices with their start and end apart: 1, of which 1 were waited for; matrix products, arithmetic and copies ran while one was open for 3% of the time, Pallas kernels for 0%

commit v1 on v0

--- a/solution.py
+++ b/solution.py
@@ -15,7 +15,21 @@
 def shards(shapes, classes, counts):
     class_f = classes.astype(jnp.float32)
     class_scale = lax.rsqrt(jnp.sum(class_f * class_f, axis=1) + epsilon)
-    piece = lax.all_gather(shapes, "cls", axis=1, tiled=True)
+    ways, here, turn = (lax.axis_size("cls"), lax.axis_index("cls"), shapes.shape[1])
+    shape = [n * ways if d == 1 else n for d, n in enumerate(shapes.shape)]
+    full = lax.dynamic_update_slice_in_dim(
+        jnp.zeros(shape, shapes.dtype), shapes, here * turn, axis=1
+    )
+    going_up = going_down = shapes
+    for far in range(1, ways // 2 + 1):
+        going_up = lax.ppermute(going_up, "cls", [(d, (d + 1) % ways) for d in range(ways)])
+        full = lax.dynamic_update_slice_in_dim(full, going_up, (here - far) % ways * turn, axis=1)
+        if 2 * far < ways:
+            going_down = lax.ppermute(going_down, "cls", [(d, (d - 1) % ways) for d in range(ways)])
+            full = lax.dynamic_update_slice_in_dim(
+                full, going_down, (here + far) % ways * turn, axis=1
+            )
+    piece = full
     term = lax.dot_general(
         piece, classes, (((1,), (1,)), ((), ())), preferred_element_type=jnp.float32
     )

time: 247 us -> 225 us (0.911)
  between operations: 13.4 us -> 0.13 us
  waiting for transfers between devices: 15.9 us -> 8.25 us
    all_gather x1 -> x0, waiting for transfers between devices: 15.2 us -> none  [shards(): piece = lax.all_gather(shapes, 'cls', axis=1, tiled=True)]
    ppermute x0 -> x3, waiting for transfers between devices: none -> 8.25 us  [the longest x2 8.25 us: shards(): lax.ppermute(going_up, 'cls', [(d, (d + 1) % ways) for d in range(ways)])]
  transfers between devices with their start and end apart: 1 -> 3, of which waited for: 1 -> 2; matrix products, arithmetic and copies ran while one was open for 3% -> 3% of each run, Pallas kernels for 0% -> 0%
where the time goes in v1:
time: 225 us; the launch traced here: 224 us
  blocking collectives  126 us (56%)
  matrix products  71.3 us (32%)
  other arithmetic  15.8 us (7%)
  waiting for transfers between devices  8.25 us (4%)
  starting transfers between devices  2.44 us (1%)
    psum x3, blocking collectives, shards(): col_scale = target / lax.psum(column_part, 'shape')  103 us
    dot_general x3, matrix products, shards(): jnp.dot(kernel, col_scale, precision=lax.Precision.HIGHEST)  34.4 us
    psum x4, blocking collectives, row_totals(): return lax.psum(partial_value, 'cls')  23 us
    dot_general x3, matrix products, shards(): column_part = jnp.dot(row_inv, kernel, precision=lax.Precision.HIGHEST)  22.9 us
    dot_general x1, matrix products, shards(): lax.dot_general(piece, classes, (((1,), (1,)), ((), ())), preferred_eleme...  14 us
    ppermute x2, waiting for transfers between devices, shards(): lax.ppermute(going_up, 'cls', [(d, (d + 1) % ways) for d in range(ways)])  8.25 us
    convert_element_type x1, other arithmetic, shards(): return result.astype(jnp.bfloat16)  8 us
    reduce_sum x1, other arithmetic, shards(): class_scale = lax.rsqrt(jnp.sum(class_f * class_f, axis=1) + epsilon)  7.35 us
  transfers between devices with their start and end apart: 3, of which 2 were waited for; matrix products, arithmetic and copies ran while one was open for 3% of the time, Pallas kernels for 0%

profile of v1, /device:TPU:0, one launch (start us, length us, event | category | flops | bytes accessed | tf_op | source)
XLA Modules:
  0.0 224.4 jit_solution(8693980870699659762)
XLA Ops:
  0.0 0.0 copy-start
  0.0 2.4 %collective-permute-start.1 = (bf16[512,320]{0,1:T(8,128)(2,1)}, bf16[512,320]{0,1:T(8,128)(2,1)S(1)}, u32[]{:S(2)}, u32[]{:S(2)}) collective-permute-start(bf16[512,320]{0,1:T(8,128)(2,1)} %param.3), channel_id=1, source_target_pairs={{0,3},{1,0},{2,1},{3,2},{4,7},{5,4},{6,5},{7,6},{8,11},{9,8},{10,9... | collective-permute-start | bytes 983048 | tf_op jit(solution)/shard_map/ppermute | solution.py:28
  2.4 0.0 collective-permute-start
  2.4 7.3 %multiply_reduce_fusion = f32[5120]{0:T(1024)S(1)} fusion(bf16[5120,1280]{1,0:T(8,128)(2,1)} %param.4), kind=kLoop, calls=%fused_computation | loop fusion | flops 19655680 | bytes 13127680 | tf_op jit(solution)/shard_map/reduce_sum | solution.py:17
  9.9 2.0 collective-permute-done
  11.8 0.0 collective-permute-start.2
  11.8 0.1 broadcast_in_dim.2
  11.9 0.0 copy-done
  12.0 0.0 collective-permute-done.1
  12.1 6.3 %collective-permute-done.2 = bf16[512,320]{0,1:T(8,128)(2,1)S(1)} collective-permute-done((bf16[512,320]{0,1:T(8,128)(2,1)S(1)}, bf16[512,320]{0,1:T(8,128)(2,1)S(1)}, u32[]{:S(2)}, u32[]{:S(2)}) %collective-permute-start.2) | collective-permute-done | bytes 327712 | tf_op jit(solution)/shard_map/ppermute | solution.py:25
  18.4 0.3 multiply_reduce_fusion.1
  18.7 14.0 %fusion = (f32[512]{0:T(512)S(1)}, f32[512,5120]{1,0:T(8,128)}) fusion(f32[5120]{0:T(1024)S(1)} %add_rsqrt_fusion, f32[512]{0:T(512)S(1)} %rsqrt_multiply_fusion, bf16[512,1280]{0,1:T(8,128)(2,1)S(1)} %constant_dynamic-update-slice_fusion, bf16[5120,1280]{1,0:T(8,128)(2,1)} %param.4), kind=kOutput, calls=%fused_computation.17 | convolution fusion | flops 6718750208 | bytes 24928256 | tf_op jit(solution)/shard_map/dot_general | solution.py:33
  32.7 0.0 copy-start.1
  32.7 5.8 %psum.49 = f32[512]{0:T(512)S(1)} all-reduce(f32[512]{0:T(512)S(1)} %get-tuple-element.5), channel_id=1, replica_groups=mesh['shape'=8,'cls'=4] {'cls'}, use_global_device_ids=true, to_apply=%region_3.4 | all-reduce | flops 512 | bytes 4096 | tf_op jit(solution)/shard_map/psum | solution.py:12
  38.5 7.6 %fusion.1 = f32[1,5120]{1,0:T(1,128)S(1)} fusion(f32[512,1]{0,1:T(1,128)S(1)} %bitcast.32, f32[512,5120]{1,0:T(8,128)} %get-tuple-element.6), kind=kOutput, calls=%fused_computation.18 | convolution fusion | flops 31457280 | bytes 10508288 | tf_op jit(solution)/shard_map/dot_general | solution.py:44
  46.1 37.4 %psum.50 = f32[5120]{0:T(1024)S(1)} all-reduce(f32[5120]{0:T(1024)S(1)} %bitcast.27), channel_id=1, replica_groups=mesh['shape'=8,'cls'=4] {'shape'}, use_global_device_ids=true, to_apply=%region_4.5 | all-reduce | flops 5120 | bytes 40960 | tf_op jit(solution)/shard_map/psum | solution.py:45
  83.5 0.0 copy-done.1
  83.5 11.5 %fusion.2 = f32[1,512]{1,0:T(1,128)S(1)} fusion(f32[512,5120]{1,0:T(8,128)} %get-tuple-element.6, f32[5120,1]{0,1:T(1,128)S(1)} %bitcast.30), kind=kOutput, calls=%fused_computation.19 | convolution fusion | flops 31457280 | bytes 10508288 | tf_op jit(solution)/shard_map/dot_general | solution.py:46
  95.0 5.7 %psum.51 = f32[512]{0:T(512)S(1)} all-reduce(f32[512]{0:T(512)S(1)} %bitcast.33), channel_id=1, replica_groups=mesh['shape'=8,'cls'=4] {'cls'}, use_global_device_ids=true, to_apply=%region_5.6 | all-reduce | flops 512 | bytes 4096 | tf_op jit(solution)/shard_map/psum | solution.py:12
  100.6 7.6 %fusion.3 = f32[1,5120]{1,0:T(1,128)S(1)} fusion(f32[512,1]{0,1:T(1,128)S(1)} %bitcast.34, f32[512,5120]{1,0:T(8,128)} %get-tuple-element.6), kind=kOutput, calls=%fused_computation.20 | convolution fusion | flops 31457280 | bytes 10508288 | tf_op jit(solution)/shard_map/dot_general | solution.py:44
  108.3 33.0 %psum.52 = f32[5120]{0:T(1024)S(1)} all-reduce(f32[5120]{0:T(1024)S(1)} %bitcast.28), channel_id=1, replica_groups=mesh['shape'=8,'cls'=4] {'shape'}, use_global_device_ids=true, to_apply=%region_6.7 | all-reduce | flops 5120 | bytes 40960 | tf_op jit(solution)/shard_map/psum | solution.py:45
  141.3 11.5 %fusion.4 = f32[1,512]{1,0:T(1,128)S(1)} fusion(f32[512,5120]{1,0:T(8,128)} %get-tuple-element.6, f32[5120,1]{0,1:T(1,128)S(1)} %bitcast.31), kind=kOutput, calls=%fused_computation.21 | convolution fusion | flops 31457280 | bytes 10508288 | tf_op jit(solution)/shard_map/dot_general | solution.py:46
  152.8 5.9 %psum.53 = f32[512]{0:T(512)S(1)} all-reduce(f32[512]{0:T(512)S(1)} %bitcast.35), channel_id=1, replica_groups=mesh['shape'=8,'cls'=4] {'cls'}, use_global_device_ids=true, to_apply=%region_7.8 | all-reduce | flops 512 | bytes 4096 | tf_op jit(solution)/shard_map/psum | solution.py:12
  158.7 7.6 %fusion.5 = f32[1,5120]{1,0:T(1,128)S(1)} fusion(f32[512,1]{0,1:T(1,128)S(1)} %bitcast.36, f32[512,5120]{1,0:T(8,128)} %get-tuple-element.6), kind=kOutput, calls=%fused_computation.22 | convolution fusion | flops 31457280 | bytes 10508288 | tf_op jit(solution)/shard_map/dot_general | solution.py:44
  166.3 33.0 %psum.54 = f32[5120]{0:T(1024)S(1)} all-reduce(f32[5120]{0:T(1024)S(1)} %bitcast.29), channel_id=1, replica_groups=mesh['shape'=8,'cls'=4] {'shape'}, use_global_device_ids=true, to_apply=%region_8.9 | all-reduce | flops 5120 | bytes 40960 | tf_op jit(solution)/shard_map/psum | solution.py:45
  199.3 11.5 %fusion.6 = f32[1,512]{1,0:T(1,128)S(1)} fusion(f32[512,5120]{1,0:T(8,128)} %get-tuple-element.6, f32[5120,1]{0,1:T(1,128)S(1)} %bitcast.26), kind=kOutput, calls=%fused_computation.23 | convolution fusion | flops 31457280 | bytes 10508288 | tf_op jit(solution)/shard_map/dot_general | solution.py:46
  210.8 5.7 %psum.55 = f32[512]{0:T(512)S(1)} all-reduce(f32[512]{0:T(512)S(1)} %bitcast.37), channel_id=1, replica_groups=mesh['shape'=8,'cls'=4] {'cls'}, use_global_device_ids=true, to_apply=%region_9.10 | all-reduce | flops 512 | bytes 4096 | tf_op jit(solution)/shard_map/psum | solution.py:12
  216.4 8.0 %multiply_convert_fusion = bf16[512,5120]{1,0:T(8,128)(2,1)} fusion(f32[512,5120]{1,0:T(8,128)} %get-tuple-element.6, f32[5120]{0:T(1024)S(1)} %convert_divide_fusion, f32[512]{0:T(512)S(1)} %broadcast_divide_fusion), kind=kLoop, calls=%fused_computation.1 | loop fusion | flops 7864320 | bytes 15751168 | tf_op jit(solution)/shard_map/convert_element_type | solution.py:48
  (13 shorter events, 0.2 us)
Async XLA Ops:
  0.0 11.9 %copy-start = (bf16[512,320]{0,1:T(8,128)(2,1)S(1)}, bf16[512,320]{0,1:T(8,128)(2,1)}, u32[]{:S(2)}) copy-start(bf16[512,320]{0,1:T(8,128)(2,1)} %param.3) | copy-start | bytes 983044
  0.0 12.0 %collective-permute-start.1 = (bf16[512,320]{0,1:T(8,128)(2,1)}, bf16[512,320]{0,1:T(8,128)(2,1)S(1)}, u32[]{:S(2)}, u32[]{:S(2)}) collective-permute-start(bf16[512,320]{0,1:T(8,128)(2,1)} %param.3), channel_id=1, source_target_pairs={{0,3},{1,0},{2,1},{3,2},{4,7},{5,4},{6,5},{7,6},{8,11},{9,8},{10,9... | collective-permute-start | bytes 983048 | tf_op jit(solution)/shard_map/ppermute | solution.py:28
  2.4 9.4 %collective-permute-start = (bf16[512,320]{0,1:T(8,128)(2,1)}, bf16[512,320]{0,1:T(8,128)(2,1)S(1)}, u32[]{:S(2)}, u32[]{:S(2)}) collective-permute-start(bf16[512,320]{0,1:T(8,128)(2,1)} %param.3), channel_id=1, source_target_pairs={{0,1},{1,2},{2,3},{3,0},{4,5},{5,6},{6,7},{7,4},{8,9},{9,10},{10,1... | collective-permute-start | bytes 983048 | tf_op jit(solution)/shard_map/ppermute | solution.py:25
  11.8 6.5 %collective-permute-start.2 = (bf16[512,320]{0,1:T(8,128)(2,1)S(1)}, bf16[512,320]{0,1:T(8,128)(2,1)S(1)}, u32[]{:S(2)}, u32[]{:S(2)}) collective-permute-start(bf16[512,320]{0,1:T(8,128)(2,1)S(1)} %collective-permute-done), channel_id=1, source_target_pairs={{0,1},{1,2},{2,3},{3,0},{4,5},{5,6},{6,7},{7,4},{8,9},{9,10},{10,1... | collective-permute-start | bytes 983048 | tf_op jit(solution)/shard_map/ppermute | solution.py:25
  32.7 50.8 %copy-start.1 = (s32[5120]{0:T(1024)S(1)}, s32[5120]{0:T(1024)}, u32[]{:S(2)}) copy-start(s32[5120]{0:T(1024)} %param.5) | copy-start | bytes 61444
